TPU v7x, 256 devices: a whole 4x4x8 slice. The times are simulated.
256 devices in a mesh: row: 16 (over z, core), col: 4 (over x), inner: 4 (over y).
Axes of the slice: x: 4, y: 4, z: 8, core: 2. Of those that a mesh axis runs over, the one named last changes fastest.
Arguments:
- density: bfloat16 [64, 16, 256, 256], P('row', ('col', 'inner')), may hold values from -1.5 to 1.5, as said below
- block_cols: int32 [64, 16], replicated, may hold values from 0 to 63, as said below
- mixing: float32 [3], replicated, may hold values from 0.02 to 1.5, as said below
Outputs:
- purified: bfloat16 [64, 16, 256, 256], P('row', ('col', 'inner'))
Inputs may be any that keep to these rules, and one draw needn't show every extreme that they name: Slot g of block row i names a block row of group g (rows g * 4 to g * 4 + 3); within one group of block rows, slot g names each row of group g once. Slot i // 4 of row i names i itself. The pattern is symmetric: row block_cols[i, g] names i in slot i // 4. It is consistent: block_cols[block_cols[i, t], g] == block_cols[i, g] for all i, t, g. `density`: block (i, g) is the transpose of block (block_cols[i, g], i // 4). `mixing`: element 0 lies in 0.5 to 1.5, elements 1 and 2 in 0.02 to 0.05.
All inputs are finite; a program needn't handle non-finite values.
Results may differ from a plain program's by a relative error of at most 0.007.
Values may be sent and summed in bfloat16 or wider, within the bound.
No kernel may reach another device: no remote copies, remote signals or barrier semaphores. Data moves between devices by JAX's collectives and lax.ppermute only.
A program may use at most 128 MiB of HBM per device.

v0:
```python
import jax
import jax.numpy as jnp
from jax import lax
from jax.experimental import pallas as pl
from jax.experimental.pallas import tpu as pltpu
from jax.sharding import PartitionSpec as P


AXES = ("row", "col", "inner")
CORES = 2
NC = 4
B = 256
PIECES = (
    *(((0, 0),), ((-1, 0),), ((1, 0),), ((2, 0),), ((0, -1),), ((0, 1),), ((0, 2),)),
    *(((-1, -1), (1, -1)), ((-1, 1), (1, 1)), ((-1, -2), (1, -2))),
    *(((2, -1),), ((2, 1),), ((2, 2),)),
)
COLUMNS = (
    *(((0, 0),), ((-1, 0),), ((-2, 0),), ((-3, 0),), ((-4, 0),)),
    *(((0, 1),), ((-1, 1),), ((-2, 1),), ((-3, 1),)),
    *(((1, 1), (1, 0), (2, 1), (2, 0)), ((3, 1), (3, 0), (4, 1))),
)
LEFTS = len(PIECES)
RIGHTS = len(COLUMNS)


def permutation(sizes, move):
    rows, cols, inners = sizes
    pairs = []
    for row in range(rows):
        for col in range(cols):
            for inner in range(inners):
                z, core = divmod(row, CORES)
                sign = 1 if core == 0 else -1
                dz, dx, dy, flip = move(sign)
                to_row = (z + dz) % (rows // CORES) * CORES + (core + flip) % CORES
                to = (to_row * cols + (col + dx) % cols) * inners + (inner + dy) % inners
                pairs.append(((row * cols + col) * inners + inner, to))
    return pairs


def product_kernel(*refs):
    cols_ref, mix_ref, own_ref = refs[:3]
    left, right = refs[3 : 3 + LEFTS], refs[3 + LEFTS : 3 + LEFTS + RIGHTS]
    s_ref, m_ref, lbuf, rbuf, lsem, rsem = refs[3 + LEFTS + RIGHTS :]
    row = lax.axis_index("row")
    x = lax.axis_index("col")
    y = lax.axis_index("inner")
    zs = lax.axis_size("row") // CORES
    xs = lax.axis_size("col")
    ys = lax.axis_size("inner")
    z = row // CORES
    core = row % CORES
    sign = 1 - 2 * core
    weight = jnp.where(row == x * ys + y, mix_ref[0], 0.0)

    def local(c, u):
        return cols_ref[c, u] - NC * u

    @pl.loop(0, NC)
    def _(c):
        a = local(c, row)
        for src, owners in zip(left, PIECES):
            for i, (first, second) in enumerate(owners):
                dx = jnp.where(core == 0, first, second)
                dy = jnp.where(core == 0, second, first)
                g = lax.rem(x + dx + xs, xs) * ys + lax.rem(y + dy + ys, ys)
                dst = lbuf.at[c, :, pl.ds(pl.multiple_of(g * B, B), B)]
                pltpu.make_async_copy(src.at[i * NC + a], dst, lsem.at[c]).start()
        for src, owners in zip(right, COLUMNS):
            for i, (hops, flip) in enumerate(owners):
                u = lax.rem(z + hops * sign + zs, zs) * CORES + (1 - core if flip else core)
                dst = rbuf.at[c, pl.ds(pl.multiple_of(u * B, B), B), :]
                pltpu.make_async_copy(src.at[i * NC + local(c, u)], dst, rsem.at[c]).start()

    @pl.loop(0, NC)
    def _(c):
        pltpu.make_async_copy(lbuf.at[c], lbuf.at[c], lsem.at[c]).wait()
        pltpu.make_async_copy(rbuf.at[c], rbuf.at[c], rsem.at[c]).wait()
        a = local(c, row)
        total = jnp.dot(lbuf[c], rbuf[c], preferred_element_type=jnp.float32)
        square = total.astype(jnp.bfloat16)
        s_ref[a] = square
        eye = lax.broadcasted_iota(jnp.int32, (B, B), 0) == lax.broadcasted_iota(
            jnp.int32, (B, B), 1
        )
        m_ref[a] = (
            jnp.where(eye, weight, 0.0)
            + mix_ref[1] * own_ref[a].astype(jnp.float32)
            + mix_ref[2] * square.astype(jnp.float32)
        ).astype(jnp.bfloat16)


def product(block_cols, mixing, own, left, right):
    tile = jax.ShapeDtypeStruct(own.shape, own.dtype)
    vmem = pl.BlockSpec(memory_space=pltpu.VMEM)
    depth = sum(len(owners) for owners in COLUMNS) * B
    return pl.pallas_call(
        product_kernel,
        out_shape=(tile, tile),
        in_specs=[pl.BlockSpec(memory_space=pltpu.SMEM)] * 2
        + [vmem]
        + [pl.BlockSpec(memory_space=pl.ANY)] * (len(left) + len(right)),
        out_specs=(vmem, vmem),
        scratch_shapes=[
            pltpu.VMEM((NC, B, depth), jnp.bfloat16),
            pltpu.VMEM((NC, depth, B), jnp.bfloat16),
            pltpu.SemaphoreType.DMA((NC,)),
            pltpu.SemaphoreType.DMA((NC,)),
        ],
        cost_estimate=pl.CostEstimate(
            flops=2 * NC * B * depth * B, bytes_accessed=4 * NC * B * depth, transcendentals=0
        ),
        name="product",
    )(block_cols, mixing, own, *left, *right)


def solution(mesh):
    sizes = tuple(mesh.shape[a] for a in AXES)
    moves = {
        "za": lambda s: (s, 0, 0, 0),
        "fa": lambda s: (0, 1, 0, 0) if s > 0 else (0, 0, 1, 0),
        "fb": lambda s: (0, -1, 0, 0) if s > 0 else (0, 0, -1, 0),
        "sa": lambda s: (0, 0, 1, 0) if s > 0 else (0, 1, 0, 0),
        "sb": lambda s: (0, 0, -1, 0) if s > 0 else (0, -1, 0, 0),
        "core": lambda s: (0, 0, 0, 1),
    }
    perms = {k: permutation(sizes, m) for k, m in moves.items()}

    def send(value, name):
        return lax.ppermute(value, AXES, perms[name])

    def panels(row_tile, col_tile):
        fa = send(row_tile, "fa")
        fb = send(row_tile, "fb")
        fc = send(fb, "fb")
        oa = send(row_tile, "sa")
        ob = send(row_tile, "sb")
        oc = send(ob, "sb")
        pair = jnp.concatenate([fa, fb])
        ra = send(pair, "sa")
        rb = send(pair, "sb")
        rc = send(ra, "sa")
        ga = send(fc, "sa")
        gb = send(fc, "sb")
        gc = send(gb, "sb")
        other = send(col_tile, "core")
        mine, theirs = [col_tile], [other]
        for _ in range(4):
            mine.append(send(mine[-1], "za"))
        for _ in range(3):
            theirs.append(send(theirs[-1], "za"))
        early = [t for pair in zip(mine[1:3], theirs[1:3]) for t in pair]
        arrived = [jnp.concatenate(early), jnp.concatenate([mine[3], theirs[3], mine[4]])]
        swapped = [send(t, "core") for t in arrived]
        left = [row_tile, fa, fb, fc, oa, ob, oc, ra, rb, rc, ga, gb, gc]
        return left, mine + theirs + swapped

    def body(density, block_cols, mixing):
        own = density[:, 0]

        def step(tiles):
            return product(block_cols, mixing, own, *panels(*tiles))

        return step(step((own, own)))[0][:, None]

    in_specs = (P("row", ("col", "inner"), None, None), P(), P())
    out_specs = P("row", ("col", "inner"), None, None)
    return jax.shard_map(body, mesh=mesh, in_specs=in_specs, out_specs=out_specs, check_vma=False)
```

profile of v0, /device:TPU:1, one launch (start us, length us, event | category | flops | bytes accessed | tf_op | source)
XLA Modules:
  0.0 195.2 jit_solution(9612962072801050548)
XLA Ops:
  0.0 6.4 %collective-permute-start.12 = (bf16[4,256,256]{2,1,0:T(8,128)(2,1)}, bf16[4,256,256]{2,1,0:T(8,128)(2,1)S(1)}, u32[]{:S(2)}, u32[]{:S(2)}) collective-permute-start(bf16[4,256,256]{2,1,0:T(8,128)(2,1)} %bitcast.4), channel_id=1, source_target_pairs={{0,32},{1,33},{2,34},{3,35},{4,36},{5,37},{6,38},{7,39},{8,40},{9,... | collective-permute-start | bytes 1572872 | tf_op jit(solution)/shard_map/ppermute | solution.py:131
  6.4 6.4 %collective-permute-done.12.refs_17_ = bf16[4,256,256]{2,1,0:T(8,128)(2,1)S(1)} collective-permute-done((bf16[4,256,256]{2,1,0:T(8,128)(2,1)}, bf16[4,256,256]{2,1,0:T(8,128)(2,1)S(1)}, u32[]{:S(2)}, u32[]{:S(2)}) %collective-permute-start.12) | collective-permute-done | bytes 524320 | tf_op jit(solution)/shard_map/ppermute | solution.py:131
  12.8 3.0 %collective-permute-start.13 = (bf16[4,256,256]{2,1,0:T(8,128)(2,1)S(1)}, bf16[4,256,256]{2,1,0:T(8,128)(2,1)S(1)}, u32[]{:S(2)}, u32[]{:S(2)}) collective-permute-start(bf16[4,256,256]{2,1,0:T(8,128)(2,1)S(1)} %collective-permute-done.12.refs_17_), channel_id=1, source_target_pairs={{0,32},{1,33},{2,34},{3,35},{4,36},{5,37},{6,38},{7,39},{8,40},{9,... | collective-permute-start | bytes 1572872 | tf_op jit(solution)/shard_map/ppermute | solution.py:131
  18.8 3.2 %collective-permute-done.13.refs_18_ = bf16[4,256,256]{2,1,0:T(8,128)(2,1)S(1)} collective-permute-done((bf16[4,256,256]{2,1,0:T(8,128)(2,1)S(1)}, bf16[4,256,256]{2,1,0:T(8,128)(2,1)S(1)}, u32[]{:S(2)}, u32[]{:S(2)}) %collective-permute-start.13) | collective-permute-done | bytes 524320 | tf_op jit(solution)/shard_map/ppermute | solution.py:131
  22.0 3.4 %collective-permute-start.14 = (bf16[4,256,256]{2,1,0:T(8,128)(2,1)S(1)}, bf16[4,256,256]{2,1,0:T(8,128)(2,1)S(1)}, u32[]{:S(2)}, u32[]{:S(2)}) collective-permute-start(bf16[4,256,256]{2,1,0:T(8,128)(2,1)S(1)} %collective-permute-done.13.refs_18_), channel_id=1, source_target_pairs={{0,32},{1,33},{2,34},{3,35},{4,36},{5,37},{6,38},{7,39},{8,40},{9,... | collective-permute-start | bytes 1572872 | tf_op jit(solution)/shard_map/ppermute | solution.py:131
  27.6 3.1 %collective-permute-start.18 = (bf16[4,256,256]{2,1,0:T(8,128)(2,1)S(1)}, bf16[4,256,256]{2,1,0:T(8,128)(2,1)S(1)}, u32[]{:S(2)}, u32[]{:S(2)}) collective-permute-start(bf16[4,256,256]{2,1,0:T(8,128)(2,1)S(1)} %collective-permute-done.17.refs_22_), channel_id=1, source_target_pairs={{0,32},{1,33},{2,34},{3,35},{4,36},{5,37},{6,38},{7,39},{8,40},{9,... | collective-permute-start | bytes 1572872 | tf_op jit(solution)/shard_map/ppermute | solution.py:131
  33.6 2.7 %collective-permute-start.15 = (bf16[4,256,256]{2,1,0:T(8,128)(2,1)S(1)}, bf16[4,256,256]{2,1,0:T(8,128)(2,1)S(1)}, u32[]{:S(2)}, u32[]{:S(2)}) collective-permute-start(bf16[4,256,256]{2,1,0:T(8,128)(2,1)S(1)} %collective-permute-done.14.refs_19_), channel_id=1, source_target_pairs={{0,32},{1,33},{2,34},{3,35},{4,36},{5,37},{6,38},{7,39},{8,40},{9,... | collective-permute-start | bytes 1572872 | tf_op jit(solution)/shard_map/ppermute | solution.py:131
  36.3 2.5 %collective-permute-done.18.refs_23_ = bf16[4,256,256]{2,1,0:T(8,128)(2,1)S(1)} collective-permute-done((bf16[4,256,256]{2,1,0:T(8,128)(2,1)S(1)}, bf16[4,256,256]{2,1,0:T(8,128)(2,1)S(1)}, u32[]{:S(2)}, u32[]{:S(2)}) %collective-permute-start.18) | collective-permute-done | bytes 524320 | tf_op jit(solution)/shard_map/ppermute | solution.py:131
  38.8 3.4 %collective-permute-start.19 = (bf16[4,256,256]{2,1,0:T(8,128)(2,1)S(1)}, bf16[4,256,256]{2,1,0:T(8,128)(2,1)S(1)}, u32[]{:S(2)}, u32[]{:S(2)}) collective-permute-start(bf16[4,256,256]{2,1,0:T(8,128)(2,1)S(1)} %collective-permute-done.18.refs_23_), channel_id=1, source_target_pairs={{0,32},{1,33},{2,34},{3,35},{4,36},{5,37},{6,38},{7,39},{8,40},{9,... | collective-permute-start | bytes 1572872 | tf_op jit(solution)/shard_map/ppermute | solution.py:131
  44.0 2.8 %collective-permute-start.2 = (bf16[4,256,256]{2,1,0:T(8,128)(2,1)S(1)}, bf16[4,256,256]{2,1,0:T(8,128)(2,1)}, u32[]{:S(2)}, u32[]{:S(2)}) collective-permute-start(bf16[4,256,256]{2,1,0:T(8,128)(2,1)S(1)} %collective-permute-done.1.refs_5_), channel_id=1, source_target_pairs={{0,12},{1,13},{2,14},{3,15},{4,0},{5,1},{6,2},{7,3},{8,4},{9,5},{1... | collective-permute-start | bytes 1572872 | tf_op jit(solution)/shard_map/ppermute | solution.py:131
  54.6 3.2 %collective-permute-start.21 = (bf16[12,256,256]{2,1,0:T(8,128)(2,1)}, bf16[12,256,256]{2,1,0:T(8,128)(2,1)}, u32[]{:S(2)}, u32[]{:S(2)}) collective-permute-start(bf16[12,256,256]{2,1,0:T(8,128)(2,1)} %pad_maximum_fusion.2), channel_id=1, source_target_pairs={{0,16},{1,17},{2,18},{3,19},{4,20},{5,21},{6,22},{7,23},{8,24},{9,... | collective-permute-start | bytes 4718600 | tf_op jit(solution)/shard_map/ppermute | solution.py:131
  57.8 12.7 %collective-permute-done.5.refs_9_ = bf16[4,256,256]{2,1,0:T(8,128)(2,1)S(1)} collective-permute-done((bf16[4,256,256]{2,1,0:T(8,128)(2,1)S(1)}, bf16[4,256,256]{2,1,0:T(8,128)(2,1)S(1)}, u32[]{:S(2)}, u32[]{:S(2)}) %collective-permute-start.5) | collective-permute-done | bytes 524320 | tf_op jit(solution)/shard_map/ppermute | solution.py:131
  70.5 3.1 %collective-permute-start.10 = (bf16[4,256,256]{2,1,0:T(8,128)(2,1)}, bf16[4,256,256]{2,1,0:T(8,128)(2,1)}, u32[]{:S(2)}, u32[]{:S(2)}) collective-permute-start(bf16[4,256,256]{2,1,0:T(8,128)(2,1)} %collective-permute-done.2.refs_6_), channel_id=1, source_target_pairs={{0,3},{1,0},{2,1},{3,2},{4,7},{5,4},{6,5},{7,6},{8,11},{9,8},{10,9... | collective-permute-start | bytes 1572872 | tf_op jit(solution)/shard_map/ppermute | solution.py:131
  73.8 6.2 %collective-permute-done.10.refs_14_ = bf16[4,256,256]{2,1,0:T(8,128)(2,1)} collective-permute-done((bf16[4,256,256]{2,1,0:T(8,128)(2,1)}, bf16[4,256,256]{2,1,0:T(8,128)(2,1)}, u32[]{:S(2)}, u32[]{:S(2)}) %collective-permute-start.10) | collective-permute-done | bytes 524320 | tf_op jit(solution)/shard_map/ppermute | solution.py:131
  80.0 3.3 %collective-permute-start.11 = (bf16[4,256,256]{2,1,0:T(8,128)(2,1)}, bf16[4,256,256]{2,1,0:T(8,128)(2,1)}, u32[]{:S(2)}, u32[]{:S(2)}) collective-permute-start(bf16[4,256,256]{2,1,0:T(8,128)(2,1)} %collective-permute-done.10.refs_14_), channel_id=1, source_target_pairs={{0,3},{1,0},{2,1},{3,2},{4,7},{5,4},{6,5},{7,6},{8,11},{9,8},{10,9... | collective-permute-start | bytes 1572872 | tf_op jit(solution)/shard_map/ppermute | solution.py:131
  84.0 10.7 %collective-permute-done.9.refs_13_ = bf16[4,256,256]{2,1,0:T(8,128)(2,1)} collective-permute-done((bf16[4,256,256]{2,1,0:T(8,128)(2,1)}, bf16[4,256,256]{2,1,0:T(8,128)(2,1)}, u32[]{:S(2)}, u32[]{:S(2)}) %collective-permute-start.9) | collective-permute-done | bytes 524320 | tf_op jit(solution)/shard_map/ppermute | solution.py:131
  96.5 9.0 %product.2 = (bf16[4,256,256]{2,1,0:T(8,128)(2,1)}, bf16[4,256,256]{2,1,0:T(8,128)(2,1)}) custom-call(s32[64,16]{1,0:T(8,128)} %copy.5.refs_0_, f32[3]{0:T(128)} %refs_1_.3, bf16[4,256,256]{2,1,0:T(8,128)(2,1)} %bitcast.10, bf16[4,256,256]{2,1,0:T(8,128)(2,1)} %bitcast.11, bf16[4,256,256]{2,1,0:T(8,128)(2,1)} %copy-done.3, bf16[4,256,256]{2,1,0:T(8,128)(2,1)} %copy-done.5, ...), custom_call_target="tpu_custom_call" | custom-call | flops 2147483648 | bytes 16777216 | tf_op jit(solution)/shard_map/product/pallas_call | solution.py:98
  105.5 3.0 %collective-permute-start.34 = (bf16[4,256,256]{2,1,0:T(8,128)(2,1)}, bf16[4,256,256]{2,1,0:T(8,128)(2,1)S(1)}, u32[]{:S(2)}, u32[]{:S(2)}) collective-permute-start(bf16[4,256,256]{2,1,0:T(8,128)(2,1)} %get-tuple-element.9.refs_16_), channel_id=1, source_target_pairs={{0,32},{1,33},{2,34},{3,35},{4,36},{5,37},{6,38},{7,39},{8,40},{9,... | collective-permute-start | bytes 1572872 | tf_op jit(solution)/shard_map/ppermute | solution.py:131
  108.5 6.4 %collective-permute-done.34.refs_17_ = bf16[4,256,256]{2,1,0:T(8,128)(2,1)S(1)} collective-permute-done((bf16[4,256,256]{2,1,0:T(8,128)(2,1)}, bf16[4,256,256]{2,1,0:T(8,128)(2,1)S(1)}, u32[]{:S(2)}, u32[]{:S(2)}) %collective-permute-start.34) | collective-permute-done | bytes 524320 | tf_op jit(solution)/shard_map/ppermute | solution.py:131
  115.0 3.0 %collective-permute-start.35 = (bf16[4,256,256]{2,1,0:T(8,128)(2,1)S(1)}, bf16[4,256,256]{2,1,0:T(8,128)(2,1)S(1)}, u32[]{:S(2)}, u32[]{:S(2)}) collective-permute-start(bf16[4,256,256]{2,1,0:T(8,128)(2,1)S(1)} %collective-permute-done.34.refs_17_), channel_id=1, source_target_pairs={{0,32},{1,33},{2,34},{3,35},{4,36},{5,37},{6,38},{7,39},{8,40},{9,... | collective-permute-start | bytes 1572872 | tf_op jit(solution)/shard_map/ppermute | solution.py:131
  120.0 4.1 %collective-permute-done.35.refs_18_ = bf16[4,256,256]{2,1,0:T(8,128)(2,1)S(1)} collective-permute-done((bf16[4,256,256]{2,1,0:T(8,128)(2,1)S(1)}, bf16[4,256,256]{2,1,0:T(8,128)(2,1)S(1)}, u32[]{:S(2)}, u32[]{:S(2)}) %collective-permute-start.35) | collective-permute-done | bytes 524320 | tf_op jit(solution)/shard_map/ppermute | solution.py:131
  124.1 3.1 %collective-permute-start.36 = (bf16[4,256,256]{2,1,0:T(8,128)(2,1)S(1)}, bf16[4,256,256]{2,1,0:T(8,128)(2,1)S(1)}, u32[]{:S(2)}, u32[]{:S(2)}) collective-permute-start(bf16[4,256,256]{2,1,0:T(8,128)(2,1)S(1)} %collective-permute-done.35.refs_18_), channel_id=1, source_target_pairs={{0,32},{1,33},{2,34},{3,35},{4,36},{5,37},{6,38},{7,39},{8,40},{9,... | collective-permute-start | bytes 1572872 | tf_op jit(solution)/shard_map/ppermute | solution.py:131
  129.7 3.4 %collective-permute-start.40 = (bf16[4,256,256]{2,1,0:T(8,128)(2,1)S(1)}, bf16[4,256,256]{2,1,0:T(8,128)(2,1)S(1)}, u32[]{:S(2)}, u32[]{:S(2)}) collective-permute-start(bf16[4,256,256]{2,1,0:T(8,128)(2,1)S(1)} %collective-permute-done.39.refs_22_), channel_id=1, source_target_pairs={{0,32},{1,33},{2,34},{3,35},{4,36},{5,37},{6,38},{7,39},{8,40},{9,... | collective-permute-start | bytes 1572872 | tf_op jit(solution)/shard_map/ppermute | solution.py:131
  138.5 2.5 %collective-permute-done.40.refs_23_ = bf16[4,256,256]{2,1,0:T(8,128)(2,1)S(1)} collective-permute-done((bf16[4,256,256]{2,1,0:T(8,128)(2,1)S(1)}, bf16[4,256,256]{2,1,0:T(8,128)(2,1)S(1)}, u32[]{:S(2)}, u32[]{:S(2)}) %collective-permute-start.40) | collective-permute-done | bytes 524320 | tf_op jit(solution)/shard_map/ppermute | solution.py:131
  141.0 3.4 %collective-permute-start.41 = (bf16[4,256,256]{2,1,0:T(8,128)(2,1)S(1)}, bf16[4,256,256]{2,1,0:T(8,128)(2,1)S(1)}, u32[]{:S(2)}, u32[]{:S(2)}) collective-permute-start(bf16[4,256,256]{2,1,0:T(8,128)(2,1)S(1)} %collective-permute-done.40.refs_23_), channel_id=1, source_target_pairs={{0,32},{1,33},{2,34},{3,35},{4,36},{5,37},{6,38},{7,39},{8,40},{9,... | collective-permute-start | bytes 1572872 | tf_op jit(solution)/shard_map/ppermute | solution.py:131
  149.3 2.9 %collective-permute-done.41.refs_24_ = bf16[4,256,256]{2,1,0:T(8,128)(2,1)S(1)} collective-permute-done((bf16[4,256,256]{2,1,0:T(8,128)(2,1)S(1)}, bf16[4,256,256]{2,1,0:T(8,128)(2,1)S(1)}, u32[]{:S(2)}, u32[]{:S(2)}) %collective-permute-start.41) | collective-permute-done | bytes 524320 | tf_op jit(solution)/shard_map/ppermute | solution.py:131
  152.4 3.7 %collective-permute-done.25.refs_7_ = bf16[4,256,256]{2,1,0:T(8,128)(2,1)S(1)} collective-permute-done((bf16[4,256,256]{2,1,0:T(8,128)(2,1)S(1)}, bf16[4,256,256]{2,1,0:T(8,128)(2,1)S(1)}, u32[]{:S(2)}, u32[]{:S(2)}) %collective-permute-start.25) | collective-permute-done | bytes 524320 | tf_op jit(solution)/shard_map/ppermute | solution.py:131
  158.8 3.1 %collective-permute-done.32.refs_14_ = bf16[4,256,256]{2,1,0:T(8,128)(2,1)S(1)} collective-permute-done((bf16[4,256,256]{2,1,0:T(8,128)(2,1)S(1)}, bf16[4,256,256]{2,1,0:T(8,128)(2,1)S(1)}, u32[]{:S(2)}, u32[]{:S(2)}) %collective-permute-start.32) | collective-permute-done | bytes 524320 | tf_op jit(solution)/shard_map/ppermute | solution.py:131
  163.1 8.3 %collective-permute-done.31.refs_13_ = bf16[4,256,256]{2,1,0:T(8,128)(2,1)S(1)} collective-permute-done((bf16[4,256,256]{2,1,0:T(8,128)(2,1)S(1)}, bf16[4,256,256]{2,1,0:T(8,128)(2,1)S(1)}, u32[]{:S(2)}, u32[]{:S(2)}) %collective-permute-start.31) | collective-permute-done | bytes 524320 | tf_op jit(solution)/shard_map/ppermute | solution.py:131
  173.1 6.6 %collective-permute-done.33.refs_15_ = bf16[4,256,256]{2,1,0:T(8,128)(2,1)S(1)} collective-permute-done((bf16[4,256,256]{2,1,0:T(8,128)(2,1)S(1)}, bf16[4,256,256]{2,1,0:T(8,128)(2,1)S(1)}, u32[]{:S(2)}, u32[]{:S(2)}) %collective-permute-start.33) | collective-permute-done | bytes 524320 | tf_op jit(solution)/shard_map/ppermute | solution.py:131
  179.7 2.9 %collective-permute-done.30.refs_12_ = bf16[8,256,256]{2,1,0:T(8,128)(2,1)S(1)} collective-permute-done((bf16[8,256,256]{2,1,0:T(8,128)(2,1)S(1)}, bf16[8,256,256]{2,1,0:T(8,128)(2,1)S(1)}, u32[]{:S(2)}, u32[]{:S(2)}) %collective-permute-start.30) | collective-permute-done | bytes 1048608 | tf_op jit(solution)/shard_map/ppermute | solution.py:131
  186.1 9.0 %product.3 = (bf16[4,256,256]{2,1,0:T(8,128)(2,1)}, bf16[4,256,256]{2,1,0:T(8,128)(2,1)}) custom-call(s32[64,16]{1,0:T(8,128)} %copy.5.refs_0_, f32[3]{0:T(128)} %refs_1_.3, bf16[4,256,256]{2,1,0:T(8,128)(2,1)} %bitcast.13, bf16[4,256,256]{2,1,0:T(8,128)(2,1)} %get-tuple-element.8.refs_3_, bf16[4,256,256]{2,1,0:T(8,128)(2,1)} %copy-done.4, ...), custom_call_target="tpu_custom_call" | custom-call | flops 2147483648 | bytes 16777216 | tf_op jit(solution)/shard_map/product/pallas_call | solution.py:98
  (145 shorter events, 43.9 us)
Async XLA Ops:
  0.0 12.8 %collective-permute-start.12 = (bf16[4,256,256]{2,1,0:T(8,128)(2,1)}, bf16[4,256,256]{2,1,0:T(8,128)(2,1)S(1)}, u32[]{:S(2)}, u32[]{:S(2)}) collective-permute-start(bf16[4,256,256]{2,1,0:T(8,128)(2,1)} %bitcast.4), channel_id=1, source_target_pairs={{0,32},{1,33},{2,34},{3,35},{4,36},{5,37},{6,38},{7,39},{8,40},{9,... | collective-permute-start | bytes 1572872 | tf_op jit(solution)/shard_map/ppermute | solution.py:131
  15.9 11.7 %collective-permute-start.17 = (bf16[4,256,256]{2,1,0:T(8,128)(2,1)S(1)}, bf16[4,256,256]{2,1,0:T(8,128)(2,1)S(1)}, u32[]{:S(2)}, u32[]{:S(2)}) collective-permute-start(bf16[4,256,256]{2,1,0:T(8,128)(2,1)S(1)} %collective-permute-done.16.refs_21_), channel_id=1, source_target_pairs={{0,32},{1,33},{2,34},{3,35},{4,36},{5,37},{6,38},{7,39},{8,40},{9,... | collective-permute-start | bytes 1572872 | tf_op jit(solution)/shard_map/ppermute | solution.py:131
  15.9 17.2 %collective-permute-start = (bf16[4,256,256]{2,1,0:T(8,128)(2,1)}, bf16[4,256,256]{2,1,0:T(8,128)(2,1)S(1)}, u32[]{:S(2)}, u32[]{:S(2)}) collective-permute-start(bf16[4,256,256]{2,1,0:T(8,128)(2,1)} %bitcast.6), channel_id=1, source_target_pairs={{0,4},{1,5},{2,6},{3,7},{4,8},{5,9},{6,10},{7,11},{8,12},{9,13},{1... | collective-permute-start | bytes 1572872 | tf_op jit(solution)/shard_map/ppermute | solution.py:131
  17.2 16.0 %collective-permute-start.1 = (bf16[4,256,256]{2,1,0:T(8,128)(2,1)}, bf16[4,256,256]{2,1,0:T(8,128)(2,1)S(1)}, u32[]{:S(2)}, u32[]{:S(2)}) collective-permute-start(bf16[4,256,256]{2,1,0:T(8,128)(2,1)} %bitcast.7), channel_id=1, source_target_pairs={{0,12},{1,13},{2,14},{3,15},{4,0},{5,1},{6,2},{7,3},{8,4},{9,5},{1... | collective-permute-start | bytes 1572872 | tf_op jit(solution)/shard_map/ppermute | solution.py:131
  22.0 11.6 %collective-permute-start.14 = (bf16[4,256,256]{2,1,0:T(8,128)(2,1)S(1)}, bf16[4,256,256]{2,1,0:T(8,128)(2,1)S(1)}, u32[]{:S(2)}, u32[]{:S(2)}) collective-permute-start(bf16[4,256,256]{2,1,0:T(8,128)(2,1)S(1)} %collective-permute-done.13.refs_18_), channel_id=1, source_target_pairs={{0,32},{1,33},{2,34},{3,35},{4,36},{5,37},{6,38},{7,39},{8,40},{9,... | collective-permute-start | bytes 1572872 | tf_op jit(solution)/shard_map/ppermute | solution.py:131
  27.6 11.2 %collective-permute-start.18 = (bf16[4,256,256]{2,1,0:T(8,128)(2,1)S(1)}, bf16[4,256,256]{2,1,0:T(8,128)(2,1)S(1)}, u32[]{:S(2)}, u32[]{:S(2)}) collective-permute-start(bf16[4,256,256]{2,1,0:T(8,128)(2,1)S(1)} %collective-permute-done.17.refs_22_), channel_id=1, source_target_pairs={{0,32},{1,33},{2,34},{3,35},{4,36},{5,37},{6,38},{7,39},{8,40},{9,... | collective-permute-start | bytes 1572872 | tf_op jit(solution)/shard_map/ppermute | solution.py:131
  30.7 13.1 %collective-permute-start.4 = (bf16[4,256,256]{2,1,0:T(8,128)(2,1)}, bf16[4,256,256]{2,1,0:T(8,128)(2,1)S(1)}, u32[]{:S(2)}, u32[]{:S(2)}) collective-permute-start(bf16[4,256,256]{2,1,0:T(8,128)(2,1)} %bitcast.8), channel_id=1, source_target_pairs={{0,3},{1,0},{2,1},{3,2},{4,7},{5,4},{6,5},{7,6},{8,11},{9,8},{10,9... | collective-permute-start | bytes 1572872 | tf_op jit(solution)/shard_map/ppermute | solution.py:131
  33.2 10.8 %collective-permute-start.3 = (bf16[4,256,256]{2,1,0:T(8,128)(2,1)}, bf16[4,256,256]{2,1,0:T(8,128)(2,1)S(1)}, u32[]{:S(2)}, u32[]{:S(2)}) collective-permute-start(bf16[4,256,256]{2,1,0:T(8,128)(2,1)} %bitcast.9), channel_id=1, source_target_pairs={{0,1},{1,2},{2,3},{3,0},{4,5},{5,6},{6,7},{7,4},{8,9},{9,10},{10,1... | collective-permute-start | bytes 1572872 | tf_op jit(solution)/shard_map/ppermute | solution.py:131
  33.3 40.3 %collective-permute-start.6 = (bf16[8,256,256]{2,1,0:T(8,128)(2,1)S(1)}, bf16[8,256,256]{2,1,0:T(8,128)(2,1)}, u32[]{:S(2)}, u32[]{:S(2)}) collective-permute-start(bf16[8,256,256]{2,1,0:T(8,128)(2,1)S(1)} %constant_dynamic-update-slice_fusion), channel_id=1, source_target_pairs={{0,1},{1,2},{2,3},{3,0},{4,5},{5,6},{6,7},{7,4},{8,9},{9,10},{10,1... | collective-permute-start | bytes 3145736 | tf_op jit(solution)/shard_map/ppermute | solution.py:131
  33.6 13.2 %collective-permute-start.15 = (bf16[4,256,256]{2,1,0:T(8,128)(2,1)S(1)}, bf16[4,256,256]{2,1,0:T(8,128)(2,1)S(1)}, u32[]{:S(2)}, u32[]{:S(2)}) collective-permute-start(bf16[4,256,256]{2,1,0:T(8,128)(2,1)S(1)} %collective-permute-done.14.refs_19_), channel_id=1, source_target_pairs={{0,32},{1,33},{2,34},{3,35},{4,36},{5,37},{6,38},{7,39},{8,40},{9,... | collective-permute-start | bytes 1572872 | tf_op jit(solution)/shard_map/ppermute | solution.py:131
  38.8 11.2 %collective-permute-start.19 = (bf16[4,256,256]{2,1,0:T(8,128)(2,1)S(1)}, bf16[4,256,256]{2,1,0:T(8,128)(2,1)S(1)}, u32[]{:S(2)}, u32[]{:S(2)}) collective-permute-start(bf16[4,256,256]{2,1,0:T(8,128)(2,1)S(1)} %collective-permute-done.18.refs_23_), channel_id=1, source_target_pairs={{0,32},{1,33},{2,34},{3,35},{4,36},{5,37},{6,38},{7,39},{8,40},{9,... | collective-permute-start | bytes 1572872 | tf_op jit(solution)/shard_map/ppermute | solution.py:131
  43.9 50.9 %collective-permute-start.20 = (bf16[16,256,256]{2,1,0:T(8,128)(2,1)}, bf16[16,256,256]{2,1,0:T(8,128)(2,1)S(1)}, u32[]{:S(2)}, u32[]{:S(2)}) collective-permute-start(bf16[16,256,256]{2,1,0:T(8,128)(2,1)} %pad_maximum_fusion), channel_id=1, source_target_pairs={{0,16},{1,17},{2,18},{3,19},{4,20},{5,21},{6,22},{7,23},{8,24},{9,... | collective-permute-start | bytes 6291464 | tf_op jit(solution)/shard_map/ppermute | solution.py:131
  46.8 26.9 %collective-permute-start.7 = (bf16[8,256,256]{2,1,0:T(8,128)(2,1)S(1)}, bf16[8,256,256]{2,1,0:T(8,128)(2,1)}, u32[]{:S(2)}, u32[]{:S(2)}) collective-permute-start(bf16[8,256,256]{2,1,0:T(8,128)(2,1)S(1)} %constant_dynamic-update-slice_fusion), channel_id=1, source_target_pairs={{0,3},{1,0},{2,1},{3,2},{4,7},{5,4},{6,5},{7,6},{8,11},{9,8},{10,9... | collective-permute-start | bytes 3145736 | tf_op jit(solution)/shard_map/ppermute | solution.py:131
  50.1 20.4 %collective-permute-start.5 = (bf16[4,256,256]{2,1,0:T(8,128)(2,1)S(1)}, bf16[4,256,256]{2,1,0:T(8,128)(2,1)S(1)}, u32[]{:S(2)}, u32[]{:S(2)}) collective-permute-start(bf16[4,256,256]{2,1,0:T(8,128)(2,1)S(1)} %collective-permute-done.4.refs_8_), channel_id=1, source_target_pairs={{0,3},{1,0},{2,1},{3,2},{4,7},{5,4},{6,5},{7,6},{8,11},{9,8},{10,9... | collective-permute-start | bytes 1572872 | tf_op jit(solution)/shard_map/ppermute | solution.py:131
  54.6 40.2 %collective-permute-start.21 = (bf16[12,256,256]{2,1,0:T(8,128)(2,1)}, bf16[12,256,256]{2,1,0:T(8,128)(2,1)}, u32[]{:S(2)}, u32[]{:S(2)}) collective-permute-start(bf16[12,256,256]{2,1,0:T(8,128)(2,1)} %pad_maximum_fusion.2), channel_id=1, source_target_pairs={{0,16},{1,17},{2,18},{3,19},{4,20},{5,21},{6,22},{7,23},{8,24},{9,... | collective-permute-start | bytes 4718600 | tf_op jit(solution)/shard_map/ppermute | solution.py:131
  73.6 21.2 %collective-permute-start.8 = (bf16[8,256,256]{2,1,0:T(8,128)(2,1)}, bf16[8,256,256]{2,1,0:T(8,128)(2,1)S(1)}, u32[]{:S(2)}, u32[]{:S(2)}) collective-permute-start(bf16[8,256,256]{2,1,0:T(8,128)(2,1)} %collective-permute-done.6.refs_10_), channel_id=1, source_target_pairs={{0,1},{1,2},{2,3},{3,0},{4,5},{5,6},{6,7},{7,4},{8,9},{9,10},{10,1... | collective-permute-start | bytes 3145736 | tf_op jit(solution)/shard_map/ppermute | solution.py:131
  73.7 21.1 %collective-permute-start.9 = (bf16[4,256,256]{2,1,0:T(8,128)(2,1)}, bf16[4,256,256]{2,1,0:T(8,128)(2,1)}, u32[]{:S(2)}, u32[]{:S(2)}) collective-permute-start(bf16[4,256,256]{2,1,0:T(8,128)(2,1)} %collective-permute-done.2.refs_6_), channel_id=1, source_target_pairs={{0,1},{1,2},{2,3},{3,0},{4,5},{5,6},{6,7},{7,4},{8,9},{9,10},{10,1... | collective-permute-start | bytes 1572872 | tf_op jit(solution)/shard_map/ppermute | solution.py:131
  80.0 14.7 %collective-permute-start.11 = (bf16[4,256,256]{2,1,0:T(8,128)(2,1)}, bf16[4,256,256]{2,1,0:T(8,128)(2,1)}, u32[]{:S(2)}, u32[]{:S(2)}) collective-permute-start(bf16[4,256,256]{2,1,0:T(8,128)(2,1)} %collective-permute-done.10.refs_14_), channel_id=1, source_target_pairs={{0,3},{1,0},{2,1},{3,2},{4,7},{5,4},{6,5},{7,6},{8,11},{9,8},{10,9... | collective-permute-start | bytes 1572872 | tf_op jit(solution)/shard_map/ppermute | solution.py:131
  118.0 11.7 %collective-permute-start.39 = (bf16[4,256,256]{2,1,0:T(8,128)(2,1)S(1)}, bf16[4,256,256]{2,1,0:T(8,128)(2,1)S(1)}, u32[]{:S(2)}, u32[]{:S(2)}) collective-permute-start(bf16[4,256,256]{2,1,0:T(8,128)(2,1)S(1)} %collective-permute-done.38.refs_21_), channel_id=1, source_target_pairs={{0,32},{1,33},{2,34},{3,35},{4,36},{5,37},{6,38},{7,39},{8,40},{9,... | collective-permute-start | bytes 1572872 | tf_op jit(solution)/shard_map/ppermute | solution.py:131
  118.1 15.1 %collective-permute-start.23 = (bf16[4,256,256]{2,1,0:T(8,128)(2,1)}, bf16[4,256,256]{2,1,0:T(8,128)(2,1)S(1)}, u32[]{:S(2)}, u32[]{:S(2)}) collective-permute-start(bf16[4,256,256]{2,1,0:T(8,128)(2,1)} %get-tuple-element.8.refs_3_), channel_id=1, source_target_pairs={{0,12},{1,13},{2,14},{3,15},{4,0},{5,1},{6,2},{7,3},{8,4},{9,5},{1... | collective-permute-start | bytes 1572872 | tf_op jit(solution)/shard_map/ppermute | solution.py:131
  120.0 15.1 %collective-permute-start.22 = (bf16[4,256,256]{2,1,0:T(8,128)(2,1)}, bf16[4,256,256]{2,1,0:T(8,128)(2,1)S(1)}, u32[]{:S(2)}, u32[]{:S(2)}) collective-permute-start(bf16[4,256,256]{2,1,0:T(8,128)(2,1)} %get-tuple-element.8.refs_3_), channel_id=1, source_target_pairs={{0,4},{1,5},{2,6},{3,7},{4,8},{5,9},{6,10},{7,11},{8,12},{9,13},{1... | collective-permute-start | bytes 1572872 | tf_op jit(solution)/shard_map/ppermute | solution.py:131
  124.1 12.3 %collective-permute-start.36 = (bf16[4,256,256]{2,1,0:T(8,128)(2,1)S(1)}, bf16[4,256,256]{2,1,0:T(8,128)(2,1)S(1)}, u32[]{:S(2)}, u32[]{:S(2)}) collective-permute-start(bf16[4,256,256]{2,1,0:T(8,128)(2,1)S(1)} %collective-permute-done.35.refs_18_), channel_id=1, source_target_pairs={{0,32},{1,33},{2,34},{3,35},{4,36},{5,37},{6,38},{7,39},{8,40},{9,... | collective-permute-start | bytes 1572872 | tf_op jit(solution)/shard_map/ppermute | solution.py:131
  129.7 11.2 %collective-permute-start.40 = (bf16[4,256,256]{2,1,0:T(8,128)(2,1)S(1)}, bf16[4,256,256]{2,1,0:T(8,128)(2,1)S(1)}, u32[]{:S(2)}, u32[]{:S(2)}) collective-permute-start(bf16[4,256,256]{2,1,0:T(8,128)(2,1)S(1)} %collective-permute-done.39.refs_22_), channel_id=1, source_target_pairs={{0,32},{1,33},{2,34},{3,35},{4,36},{5,37},{6,38},{7,39},{8,40},{9,... | collective-permute-start | bytes 1572872 | tf_op jit(solution)/shard_map/ppermute | solution.py:131
  133.1 13.4 %collective-permute-start.26 = (bf16[4,256,256]{2,1,0:T(8,128)(2,1)}, bf16[4,256,256]{2,1,0:T(8,128)(2,1)S(1)}, u32[]{:S(2)}, u32[]{:S(2)}) collective-permute-start(bf16[4,256,256]{2,1,0:T(8,128)(2,1)} %get-tuple-element.8.refs_3_), channel_id=1, source_target_pairs={{0,3},{1,0},{2,1},{3,2},{4,7},{5,4},{6,5},{7,6},{8,11},{9,8},{10,9... | collective-permute-start | bytes 1572872 | tf_op jit(solution)/shard_map/ppermute | solution.py:131
  133.2 13.7 %collective-permute-start.24 = (bf16[4,256,256]{2,1,0:T(8,128)(2,1)S(1)}, bf16[4,256,256]{2,1,0:T(8,128)(2,1)S(1)}, u32[]{:S(2)}, u32[]{:S(2)}) collective-permute-start(bf16[4,256,256]{2,1,0:T(8,128)(2,1)S(1)} %collective-permute-done.23.refs_5_), channel_id=1, source_target_pairs={{0,12},{1,13},{2,14},{3,15},{4,0},{5,1},{6,2},{7,3},{8,4},{9,5},{1... | collective-permute-start | bytes 1572872 | tf_op jit(solution)/shard_map/ppermute | solution.py:131
  135.1 27.9 %collective-permute-start.28 = (bf16[8,256,256]{2,1,0:T(8,128)(2,1)S(1)}, bf16[8,256,256]{2,1,0:T(8,128)(2,1)S(1)}, u32[]{:S(2)}, u32[]{:S(2)}) collective-permute-start(bf16[8,256,256]{2,1,0:T(8,128)(2,1)S(1)} %constant_dynamic-update-slice_fusion.2), channel_id=1, source_target_pairs={{0,1},{1,2},{2,3},{3,0},{4,5},{5,6},{6,7},{7,4},{8,9},{9,10},{10,1... | collective-permute-start | bytes 3145736 | tf_op jit(solution)/shard_map/ppermute | solution.py:131
  136.4 11.5 %collective-permute-start.37 = (bf16[4,256,256]{2,1,0:T(8,128)(2,1)S(1)}, bf16[4,256,256]{2,1,0:T(8,128)(2,1)S(1)}, u32[]{:S(2)}, u32[]{:S(2)}) collective-permute-start(bf16[4,256,256]{2,1,0:T(8,128)(2,1)S(1)} %collective-permute-done.36.refs_19_), channel_id=1, source_target_pairs={{0,32},{1,33},{2,34},{3,35},{4,36},{5,37},{6,38},{7,39},{8,40},{9,... | collective-permute-start | bytes 1572872 | tf_op jit(solution)/shard_map/ppermute | solution.py:131
  141.0 11.2 %collective-permute-start.41 = (bf16[4,256,256]{2,1,0:T(8,128)(2,1)S(1)}, bf16[4,256,256]{2,1,0:T(8,128)(2,1)S(1)}, u32[]{:S(2)}, u32[]{:S(2)}) collective-permute-start(bf16[4,256,256]{2,1,0:T(8,128)(2,1)S(1)} %collective-permute-done.40.refs_23_), channel_id=1, source_target_pairs={{0,32},{1,33},{2,34},{3,35},{4,36},{5,37},{6,38},{7,39},{8,40},{9,... | collective-permute-start | bytes 1572872 | tf_op jit(solution)/shard_map/ppermute | solution.py:131
  146.8 37.9 %collective-permute-start.42 = (bf16[16,256,256]{2,1,0:T(8,128)(2,1)S(1)}, bf16[16,256,256]{2,1,0:T(8,128)(2,1)S(1)}, u32[]{:S(2)}, u32[]{:S(2)}) collective-permute-start(bf16[16,256,256]{2,1,0:T(8,128)(2,1)S(1)} %pad_maximum_fusion.1), channel_id=1, source_target_pairs={{0,16},{1,17},{2,18},{3,19},{4,20},{5,21},{6,22},{7,23},{8,24},{9,... | collective-permute-start | bytes 6291464 | tf_op jit(solution)/shard_map/ppermute | solution.py:131
  156.1 26.6 %collective-permute-start.43 = (bf16[12,256,256]{2,1,0:T(8,128)(2,1)S(1)}, bf16[12,256,256]{2,1,0:T(8,128)(2,1)S(1)}, u32[]{:S(2)}, u32[]{:S(2)}) collective-permute-start(bf16[12,256,256]{2,1,0:T(8,128)(2,1)S(1)} %pad_maximum_fusion.3), channel_id=1, source_target_pairs={{0,16},{1,17},{2,18},{3,19},{4,20},{5,21},{6,22},{7,23},{8,24},{9,... | collective-permute-start | bytes 4718600 | tf_op jit(solution)/shard_map/ppermute | solution.py:131
  158.2 14.9 %collective-permute-start.29 = (bf16[8,256,256]{2,1,0:T(8,128)(2,1)S(1)}, bf16[8,256,256]{2,1,0:T(8,128)(2,1)S(1)}, u32[]{:S(2)}, u32[]{:S(2)}) collective-permute-start(bf16[8,256,256]{2,1,0:T(8,128)(2,1)S(1)} %constant_dynamic-update-slice_fusion.2), channel_id=1, source_target_pairs={{0,3},{1,0},{2,1},{3,2},{4,7},{5,4},{6,5},{7,6},{8,11},{9,8},{10,9... | collective-permute-start | bytes 3145736 | tf_op jit(solution)/shard_map/ppermute | solution.py:131
  163.0 19.6 %collective-permute-start.30 = (bf16[8,256,256]{2,1,0:T(8,128)(2,1)S(1)}, bf16[8,256,256]{2,1,0:T(8,128)(2,1)S(1)}, u32[]{:S(2)}, u32[]{:S(2)}) collective-permute-start(bf16[8,256,256]{2,1,0:T(8,128)(2,1)S(1)} %collective-permute-done.28.refs_10_), channel_id=1, source_target_pairs={{0,1},{1,2},{2,3},{3,0},{4,5},{5,6},{6,7},{7,4},{8,9},{9,10},{10,1... | collective-permute-start | bytes 3145736 | tf_op jit(solution)/shard_map/ppermute | solution.py:131
  (51 other events, 743.1 us)
where the time goes:
time: 198 us; the launch traced here: 195 us
  waiting for transfers between devices  91.2 us (46%)
  starting transfers between devices  76.1 us (38%)
  Pallas kernels  18 us (9%)
  local copies, waits for them, and re-layouts  6 us (3%)
  other arithmetic  3.37 us (2%)
    ppermute x44, waiting for transfers between devices, send(): return lax.ppermute(value, AXES, perms[name])  91.2 us
    ppermute x44, starting transfers between devices, send(): return lax.ppermute(value, AXES, perms[name])  76.1 us
    pallas_call x2, Pallas kernels, product(): pl.pallas_call(product_kernel, out_shape=(tile, tile), in_specs=[pl.Block...  18 us
    unnamed x81, local copies, waits for them, and re-layouts  5.92 us
  transfers between devices with their start and end apart: 44, of which 22 were waited for; matrix products, arithmetic and copies ran while one was open for 2% of the time, Pallas kernels for 0%

commit v1 on v0

--- a/solution.py
+++ b/solution.py
@@ -1,3 +1,5 @@
+import functools
+
 import jax
 import jax.numpy as jnp
 from jax import lax
@@ -39,10 +41,10 @@
     return pairs
 
 
-def product_kernel(*refs):
+def product_kernel(last, *refs):
     cols_ref, mix_ref, own_ref = refs[:3]
     left, right = refs[3 : 3 + LEFTS], refs[3 + LEFTS : 3 + LEFTS + RIGHTS]
-    s_ref, m_ref, lbuf, rbuf, lsem, rsem = refs[3 + LEFTS + RIGHTS :]
+    s_ref, *m_refs, lbuf, rbuf, lsem, rsem = refs[3 + LEFTS + RIGHTS :]
     row = lax.axis_index("row")
     x = lax.axis_index("col")
     y = lax.axis_index("inner")
@@ -81,27 +83,29 @@
         total = jnp.dot(lbuf[c], rbuf[c], preferred_element_type=jnp.float32)
         square = total.astype(jnp.bfloat16)
         s_ref[a] = square
+        if last:
+            return
         eye = lax.broadcasted_iota(jnp.int32, (B, B), 0) == lax.broadcasted_iota(
             jnp.int32, (B, B), 1
         )
-        m_ref[a] = (
+        m_refs[0][a] = (
             jnp.where(eye, weight, 0.0)
             + mix_ref[1] * own_ref[a].astype(jnp.float32)
             + mix_ref[2] * square.astype(jnp.float32)
         ).astype(jnp.bfloat16)
 
 
-def product(block_cols, mixing, own, left, right):
+def product(last, block_cols, mixing, own, left, right):
     tile = jax.ShapeDtypeStruct(own.shape, own.dtype)
     vmem = pl.BlockSpec(memory_space=pltpu.VMEM)
     depth = sum(len(owners) for owners in COLUMNS) * B
     return pl.pallas_call(
-        product_kernel,
-        out_shape=(tile, tile),
+        functools.partial(product_kernel, last),
+        out_shape=(tile,) if last else (tile, tile),
         in_specs=[pl.BlockSpec(memory_space=pltpu.SMEM)] * 2
         + [vmem]
         + [pl.BlockSpec(memory_space=pl.ANY)] * (len(left) + len(right)),
-        out_specs=(vmem, vmem),
+        out_specs=(vmem,) if last else (vmem, vmem),
         scratch_shapes=[
             pltpu.VMEM((NC, B, depth), jnp.bfloat16),
             pltpu.VMEM((NC, depth, B), jnp.bfloat16),
@@ -159,10 +163,10 @@
     def body(density, block_cols, mixing):
         own = density[:, 0]
 
-        def step(tiles):
-            return product(block_cols, mixing, own, *panels(*tiles))
+        def step(n, tiles):
+            return product(n == 1, block_cols, mixing, own, *panels(*tiles))
 
-        return step(step((own, own)))[0][:, None]
+        return step(1, step(0, (own, own)))[0][:, None]
 
     in_specs = (P("row", ("col", "inner"), None, None), P(), P())
     out_specs = P("row", ("col", "inner"), None, None)

time: 198 us -> 198 us (level)
  no operation moved by 1% of the time
where the time goes in v1:
time: 198 us; the launch traced here: 195 us
  waiting for transfers between devices  91.1 us (46%)
  starting transfers between devices  76.1 us (38%)
  Pallas kernels  17.8 us (9%)
  local copies, waits for them, and re-layouts  5.97 us (3%)
  other arithmetic  3.36 us (2%)
    ppermute x44, waiting for transfers between devices, send(): return lax.ppermute(value, AXES, perms[name])  91.1 us
    ppermute x44, starting transfers between devices, send(): return lax.ppermute(value, AXES, perms[name])  76.1 us
    pallas_call x2, Pallas kernels, product(): pl.pallas_call(functools.partial(product_kernel, last), out_shape=(tile,)...  17.8 us
    unnamed x81, local copies, waits for them, and re-layouts  5.89 us
  transfers between devices with their start and end apart: 44, of which 22 were waited for; matrix products, arithmetic and copies ran while one was open for 2% of the time, Pallas kernels for 0%

profile of v1, /device:TPU:1, one launch (start us, length us, event | category | flops | bytes accessed | tf_op | source)
XLA Modules:
  0.0 194.8 jit_solution(5243764646339565924)
XLA Ops:
  0.0 6.4 %collective-permute-start.12 = (bf16[4,256,256]{2,1,0:T(8,128)(2,1)}, bf16[4,256,256]{2,1,0:T(8,128)(2,1)S(1)}, u32[]{:S(2)}, u32[]{:S(2)}) collective-permute-start(bf16[4,256,256]{2,1,0:T(8,128)(2,1)} %bitcast.4), channel_id=1, source_target_pairs={{0,32},{1,33},{2,34},{3,35},{4,36},{5,37},{6,38},{7,39},{8,40},{9,... | collective-permute-start | bytes 1572872 | tf_op jit(solution)/shard_map/ppermute | solution.py:135
  6.4 6.4 %collective-permute-done.12.refs_17_ = bf16[4,256,256]{2,1,0:T(8,128)(2,1)S(1)} collective-permute-done((bf16[4,256,256]{2,1,0:T(8,128)(2,1)}, bf16[4,256,256]{2,1,0:T(8,128)(2,1)S(1)}, u32[]{:S(2)}, u32[]{:S(2)}) %collective-permute-start.12) | collective-permute-done | bytes 524320 | tf_op jit(solution)/shard_map/ppermute | solution.py:135
  12.8 3.0 %collective-permute-start.13 = (bf16[4,256,256]{2,1,0:T(8,128)(2,1)S(1)}, bf16[4,256,256]{2,1,0:T(8,128)(2,1)S(1)}, u32[]{:S(2)}, u32[]{:S(2)}) collective-permute-start(bf16[4,256,256]{2,1,0:T(8,128)(2,1)S(1)} %collective-permute-done.12.refs_17_), channel_id=1, source_target_pairs={{0,32},{1,33},{2,34},{3,35},{4,36},{5,37},{6,38},{7,39},{8,40},{9,... | collective-permute-start | bytes 1572872 | tf_op jit(solution)/shard_map/ppermute | solution.py:135
  18.8 3.2 %collective-permute-done.13.refs_18_ = bf16[4,256,256]{2,1,0:T(8,128)(2,1)S(1)} collective-permute-done((bf16[4,256,256]{2,1,0:T(8,128)(2,1)S(1)}, bf16[4,256,256]{2,1,0:T(8,128)(2,1)S(1)}, u32[]{:S(2)}, u32[]{:S(2)}) %collective-permute-start.13) | collective-permute-done | bytes 524320 | tf_op jit(solution)/shard_map/ppermute | solution.py:135
  22.0 3.4 %collective-permute-start.14 = (bf16[4,256,256]{2,1,0:T(8,128)(2,1)S(1)}, bf16[4,256,256]{2,1,0:T(8,128)(2,1)S(1)}, u32[]{:S(2)}, u32[]{:S(2)}) collective-permute-start(bf16[4,256,256]{2,1,0:T(8,128)(2,1)S(1)} %collective-permute-done.13.refs_18_), channel_id=1, source_target_pairs={{0,32},{1,33},{2,34},{3,35},{4,36},{5,37},{6,38},{7,39},{8,40},{9,... | collective-permute-start | bytes 1572872 | tf_op jit(solution)/shard_map/ppermute | solution.py:135
  27.6 3.1 %collective-permute-start.18 = (bf16[4,256,256]{2,1,0:T(8,128)(2,1)S(1)}, bf16[4,256,256]{2,1,0:T(8,128)(2,1)S(1)}, u32[]{:S(2)}, u32[]{:S(2)}) collective-permute-start(bf16[4,256,256]{2,1,0:T(8,128)(2,1)S(1)} %collective-permute-done.17.refs_22_), channel_id=1, source_target_pairs={{0,32},{1,33},{2,34},{3,35},{4,36},{5,37},{6,38},{7,39},{8,40},{9,... | collective-permute-start | bytes 1572872 | tf_op jit(solution)/shard_map/ppermute | solution.py:135
  33.6 2.7 %collective-permute-start.15 = (bf16[4,256,256]{2,1,0:T(8,128)(2,1)S(1)}, bf16[4,256,256]{2,1,0:T(8,128)(2,1)S(1)}, u32[]{:S(2)}, u32[]{:S(2)}) collective-permute-start(bf16[4,256,256]{2,1,0:T(8,128)(2,1)S(1)} %collective-permute-done.14.refs_19_), channel_id=1, source_target_pairs={{0,32},{1,33},{2,34},{3,35},{4,36},{5,37},{6,38},{7,39},{8,40},{9,... | collective-permute-start | bytes 1572872 | tf_op jit(solution)/shard_map/ppermute | solution.py:135
  36.3 2.5 %collective-permute-done.18.refs_23_ = bf16[4,256,256]{2,1,0:T(8,128)(2,1)S(1)} collective-permute-done((bf16[4,256,256]{2,1,0:T(8,128)(2,1)S(1)}, bf16[4,256,256]{2,1,0:T(8,128)(2,1)S(1)}, u32[]{:S(2)}, u32[]{:S(2)}) %collective-permute-start.18) | collective-permute-done | bytes 524320 | tf_op jit(solution)/shard_map/ppermute | solution.py:135
  38.8 3.4 %collective-permute-start.19 = (bf16[4,256,256]{2,1,0:T(8,128)(2,1)S(1)}, bf16[4,256,256]{2,1,0:T(8,128)(2,1)S(1)}, u32[]{:S(2)}, u32[]{:S(2)}) collective-permute-start(bf16[4,256,256]{2,1,0:T(8,128)(2,1)S(1)} %collective-permute-done.18.refs_23_), channel_id=1, source_target_pairs={{0,32},{1,33},{2,34},{3,35},{4,36},{5,37},{6,38},{7,39},{8,40},{9,... | collective-permute-start | bytes 1572872 | tf_op jit(solution)/shard_map/ppermute | solution.py:135
  44.0 2.8 %collective-permute-start.2 = (bf16[4,256,256]{2,1,0:T(8,128)(2,1)S(1)}, bf16[4,256,256]{2,1,0:T(8,128)(2,1)}, u32[]{:S(2)}, u32[]{:S(2)}) collective-permute-start(bf16[4,256,256]{2,1,0:T(8,128)(2,1)S(1)} %collective-permute-done.1.refs_5_), channel_id=1, source_target_pairs={{0,12},{1,13},{2,14},{3,15},{4,0},{5,1},{6,2},{7,3},{8,4},{9,5},{1... | collective-permute-start | bytes 1572872 | tf_op jit(solution)/shard_map/ppermute | solution.py:135
  54.6 3.2 %collective-permute-start.21 = (bf16[12,256,256]{2,1,0:T(8,128)(2,1)}, bf16[12,256,256]{2,1,0:T(8,128)(2,1)}, u32[]{:S(2)}, u32[]{:S(2)}) collective-permute-start(bf16[12,256,256]{2,1,0:T(8,128)(2,1)} %pad_maximum_fusion.2), channel_id=1, source_target_pairs={{0,16},{1,17},{2,18},{3,19},{4,20},{5,21},{6,22},{7,23},{8,24},{9,... | collective-permute-start | bytes 4718600 | tf_op jit(solution)/shard_map/ppermute | solution.py:135
  57.8 12.7 %collective-permute-done.5.refs_9_ = bf16[4,256,256]{2,1,0:T(8,128)(2,1)S(1)} collective-permute-done((bf16[4,256,256]{2,1,0:T(8,128)(2,1)S(1)}, bf16[4,256,256]{2,1,0:T(8,128)(2,1)S(1)}, u32[]{:S(2)}, u32[]{:S(2)}) %collective-permute-start.5) | collective-permute-done | bytes 524320 | tf_op jit(solution)/shard_map/ppermute | solution.py:135
  70.5 3.1 %collective-permute-start.10 = (bf16[4,256,256]{2,1,0:T(8,128)(2,1)}, bf16[4,256,256]{2,1,0:T(8,128)(2,1)}, u32[]{:S(2)}, u32[]{:S(2)}) collective-permute-start(bf16[4,256,256]{2,1,0:T(8,128)(2,1)} %collective-permute-done.2.refs_6_), channel_id=1, source_target_pairs={{0,3},{1,0},{2,1},{3,2},{4,7},{5,4},{6,5},{7,6},{8,11},{9,8},{10,9... | collective-permute-start | bytes 1572872 | tf_op jit(solution)/shard_map/ppermute | solution.py:135
  73.8 6.2 %collective-permute-done.10.refs_14_ = bf16[4,256,256]{2,1,0:T(8,128)(2,1)} collective-permute-done((bf16[4,256,256]{2,1,0:T(8,128)(2,1)}, bf16[4,256,256]{2,1,0:T(8,128)(2,1)}, u32[]{:S(2)}, u32[]{:S(2)}) %collective-permute-start.10) | collective-permute-done | bytes 524320 | tf_op jit(solution)/shard_map/ppermute | solution.py:135
  80.0 3.3 %collective-permute-start.11 = (bf16[4,256,256]{2,1,0:T(8,128)(2,1)}, bf16[4,256,256]{2,1,0:T(8,128)(2,1)}, u32[]{:S(2)}, u32[]{:S(2)}) collective-permute-start(bf16[4,256,256]{2,1,0:T(8,128)(2,1)} %collective-permute-done.10.refs_14_), channel_id=1, source_target_pairs={{0,3},{1,0},{2,1},{3,2},{4,7},{5,4},{6,5},{7,6},{8,11},{9,8},{10,9... | collective-permute-start | bytes 1572872 | tf_op jit(solution)/shard_map/ppermute | solution.py:135
  84.0 10.7 %collective-permute-done.9.refs_13_ = bf16[4,256,256]{2,1,0:T(8,128)(2,1)} collective-permute-done((bf16[4,256,256]{2,1,0:T(8,128)(2,1)}, bf16[4,256,256]{2,1,0:T(8,128)(2,1)}, u32[]{:S(2)}, u32[]{:S(2)}) %collective-permute-start.9) | collective-permute-done | bytes 524320 | tf_op jit(solution)/shard_map/ppermute | solution.py:135
  96.5 9.0 %product.2 = (bf16[4,256,256]{2,1,0:T(8,128)(2,1)}, bf16[4,256,256]{2,1,0:T(8,128)(2,1)}) custom-call(s32[64,16]{1,0:T(8,128)} %copy.5.refs_0_, f32[3]{0:T(128)} %refs_1_.3, bf16[4,256,256]{2,1,0:T(8,128)(2,1)} %bitcast.10, bf16[4,256,256]{2,1,0:T(8,128)(2,1)} %bitcast.11, bf16[4,256,256]{2,1,0:T(8,128)(2,1)} %copy-done.2, bf16[4,256,256]{2,1,0:T(8,128)(2,1)} %copy-done.4, ...), custom_call_target="tpu_custom_call" | custom-call | flops 2147483648 | bytes 16777216 | tf_op jit(solution)/shard_map/product/pallas_call | solution.py:102
  105.4 2.9 %collective-permute-start.34 = (bf16[4,256,256]{2,1,0:T(8,128)(2,1)}, bf16[4,256,256]{2,1,0:T(8,128)(2,1)S(1)}, u32[]{:S(2)}, u32[]{:S(2)}) collective-permute-start(bf16[4,256,256]{2,1,0:T(8,128)(2,1)} %get-tuple-element.8.refs_16_), channel_id=1, source_target_pairs={{0,32},{1,33},{2,34},{3,35},{4,36},{5,37},{6,38},{7,39},{8,40},{9,... | collective-permute-start | bytes 1572872 | tf_op jit(solution)/shard_map/ppermute | solution.py:135
  108.3 6.4 %collective-permute-done.34.refs_17_ = bf16[4,256,256]{2,1,0:T(8,128)(2,1)S(1)} collective-permute-done((bf16[4,256,256]{2,1,0:T(8,128)(2,1)}, bf16[4,256,256]{2,1,0:T(8,128)(2,1)S(1)}, u32[]{:S(2)}, u32[]{:S(2)}) %collective-permute-start.34) | collective-permute-done | bytes 524320 | tf_op jit(solution)/shard_map/ppermute | solution.py:135
  114.8 3.0 %collective-permute-start.35 = (bf16[4,256,256]{2,1,0:T(8,128)(2,1)S(1)}, bf16[4,256,256]{2,1,0:T(8,128)(2,1)S(1)}, u32[]{:S(2)}, u32[]{:S(2)}) collective-permute-start(bf16[4,256,256]{2,1,0:T(8,128)(2,1)S(1)} %collective-permute-done.34.refs_17_), channel_id=1, source_target_pairs={{0,32},{1,33},{2,34},{3,35},{4,36},{5,37},{6,38},{7,39},{8,40},{9,... | collective-permute-start | bytes 1572872 | tf_op jit(solution)/shard_map/ppermute | solution.py:135
  119.7 4.2 %collective-permute-done.35.refs_18_ = bf16[4,256,256]{2,1,0:T(8,128)(2,1)S(1)} collective-permute-done((bf16[4,256,256]{2,1,0:T(8,128)(2,1)S(1)}, bf16[4,256,256]{2,1,0:T(8,128)(2,1)S(1)}, u32[]{:S(2)}, u32[]{:S(2)}) %collective-permute-start.35) | collective-permute-done | bytes 524320 | tf_op jit(solution)/shard_map/ppermute | solution.py:135
  123.9 3.1 %collective-permute-start.36 = (bf16[4,256,256]{2,1,0:T(8,128)(2,1)S(1)}, bf16[4,256,256]{2,1,0:T(8,128)(2,1)S(1)}, u32[]{:S(2)}, u32[]{:S(2)}) collective-permute-start(bf16[4,256,256]{2,1,0:T(8,128)(2,1)S(1)} %collective-permute-done.35.refs_18_), channel_id=1, source_target_pairs={{0,32},{1,33},{2,34},{3,35},{4,36},{5,37},{6,38},{7,39},{8,40},{9,... | collective-permute-start | bytes 1572872 | tf_op jit(solution)/shard_map/ppermute | solution.py:135
  129.5 3.4 %collective-permute-start.40 = (bf16[4,256,256]{2,1,0:T(8,128)(2,1)S(1)}, bf16[4,256,256]{2,1,0:T(8,128)(2,1)S(1)}, u32[]{:S(2)}, u32[]{:S(2)}) collective-permute-start(bf16[4,256,256]{2,1,0:T(8,128)(2,1)S(1)} %collective-permute-done.39.refs_22_), channel_id=1, source_target_pairs={{0,32},{1,33},{2,34},{3,35},{4,36},{5,37},{6,38},{7,39},{8,40},{9,... | collective-permute-start | bytes 1572872 | tf_op jit(solution)/shard_map/ppermute | solution.py:135
  138.3 2.5 %collective-permute-done.40.refs_23_ = bf16[4,256,256]{2,1,0:T(8,128)(2,1)S(1)} collective-permute-done((bf16[4,256,256]{2,1,0:T(8,128)(2,1)S(1)}, bf16[4,256,256]{2,1,0:T(8,128)(2,1)S(1)}, u32[]{:S(2)}, u32[]{:S(2)}) %collective-permute-start.40) | collective-permute-done | bytes 524320 | tf_op jit(solution)/shard_map/ppermute | solution.py:135
  140.8 3.4 %collective-permute-start.41 = (bf16[4,256,256]{2,1,0:T(8,128)(2,1)S(1)}, bf16[4,256,256]{2,1,0:T(8,128)(2,1)S(1)}, u32[]{:S(2)}, u32[]{:S(2)}) collective-permute-start(bf16[4,256,256]{2,1,0:T(8,128)(2,1)S(1)} %collective-permute-done.40.refs_23_), channel_id=1, source_target_pairs={{0,32},{1,33},{2,34},{3,35},{4,36},{5,37},{6,38},{7,39},{8,40},{9,... | collective-permute-start | bytes 1572872 | tf_op jit(solution)/shard_map/ppermute | solution.py:135
  148.9 3.0 %collective-permute-done.41.refs_24_ = bf16[4,256,256]{2,1,0:T(8,128)(2,1)S(1)} collective-permute-done((bf16[4,256,256]{2,1,0:T(8,128)(2,1)S(1)}, bf16[4,256,256]{2,1,0:T(8,128)(2,1)S(1)}, u32[]{:S(2)}, u32[]{:S(2)}) %collective-permute-start.41) | collective-permute-done | bytes 524320 | tf_op jit(solution)/shard_map/ppermute | solution.py:135
  152.2 3.6 %collective-permute-done.25.refs_7_ = bf16[4,256,256]{2,1,0:T(8,128)(2,1)S(1)} collective-permute-done((bf16[4,256,256]{2,1,0:T(8,128)(2,1)S(1)}, bf16[4,256,256]{2,1,0:T(8,128)(2,1)S(1)}, u32[]{:S(2)}, u32[]{:S(2)}) %collective-permute-start.25) | collective-permute-done | bytes 524320 | tf_op jit(solution)/shard_map/ppermute | solution.py:135
  158.7 2.9 %collective-permute-done.32.refs_14_ = bf16[4,256,256]{2,1,0:T(8,128)(2,1)S(1)} collective-permute-done((bf16[4,256,256]{2,1,0:T(8,128)(2,1)S(1)}, bf16[4,256,256]{2,1,0:T(8,128)(2,1)S(1)}, u32[]{:S(2)}, u32[]{:S(2)}) %collective-permute-start.32) | collective-permute-done | bytes 524320 | tf_op jit(solution)/shard_map/ppermute | solution.py:135
  162.9 8.3 %collective-permute-done.31.refs_13_ = bf16[4,256,256]{2,1,0:T(8,128)(2,1)S(1)} collective-permute-done((bf16[4,256,256]{2,1,0:T(8,128)(2,1)S(1)}, bf16[4,256,256]{2,1,0:T(8,128)(2,1)S(1)}, u32[]{:S(2)}, u32[]{:S(2)}) %collective-permute-start.31) | collective-permute-done | bytes 524320 | tf_op jit(solution)/shard_map/ppermute | solution.py:135
  172.9 6.6 %collective-permute-done.33.refs_15_ = bf16[4,256,256]{2,1,0:T(8,128)(2,1)S(1)} collective-permute-done((bf16[4,256,256]{2,1,0:T(8,128)(2,1)S(1)}, bf16[4,256,256]{2,1,0:T(8,128)(2,1)S(1)}, u32[]{:S(2)}, u32[]{:S(2)}) %collective-permute-start.33) | collective-permute-done | bytes 524320 | tf_op jit(solution)/shard_map/ppermute | solution.py:135
  179.5 2.9 %collective-permute-done.30.refs_12_ = bf16[8,256,256]{2,1,0:T(8,128)(2,1)S(1)} collective-permute-done((bf16[8,256,256]{2,1,0:T(8,128)(2,1)S(1)}, bf16[8,256,256]{2,1,0:T(8,128)(2,1)S(1)}, u32[]{:S(2)}, u32[]{:S(2)}) %collective-permute-start.30) | collective-permute-done | bytes 1048608 | tf_op jit(solution)/shard_map/ppermute | solution.py:135
  185.9 8.8 %product.3 = bf16[4,256,256]{2,1,0:T(8,128)(2,1)} custom-call(s32[64,16]{1,0:T(8,128)} %copy.5.refs_0_, f32[3]{0:T(128)} %refs_1_.3, bf16[4,256,256]{2,1,0:T(8,128)(2,1)} %bitcast.13, bf16[4,256,256]{2,1,0:T(8,128)(2,1)} %get-tuple-element.7.refs_3_, bf16[4,256,256]{2,1,0:T(8,128)(2,1)} %copy-done.5, bf16[4,256,256]{2,1,0:T(8,128)(2,1)} %copy-done.3, ...), custom_call_target="tpu_custom_call" | custom-call | flops 2147483648 | bytes 16777216 | tf_op jit(solution)/shard_map/product/pallas_call | solution.py:102
  (145 shorter events, 43.9 us)
Async XLA Ops:
  0.0 12.8 %collective-permute-start.12 = (bf16[4,256,256]{2,1,0:T(8,128)(2,1)}, bf16[4,256,256]{2,1,0:T(8,128)(2,1)S(1)}, u32[]{:S(2)}, u32[]{:S(2)}) collective-permute-start(bf16[4,256,256]{2,1,0:T(8,128)(2,1)} %bitcast.4), channel_id=1, source_target_pairs={{0,32},{1,33},{2,34},{3,35},{4,36},{5,37},{6,38},{7,39},{8,40},{9,... | collective-permute-start | bytes 1572872 | tf_op jit(solution)/shard_map/ppermute | solution.py:135
  15.9 11.7 %collective-permute-start.17 = (bf16[4,256,256]{2,1,0:T(8,128)(2,1)S(1)}, bf16[4,256,256]{2,1,0:T(8,128)(2,1)S(1)}, u32[]{:S(2)}, u32[]{:S(2)}) collective-permute-start(bf16[4,256,256]{2,1,0:T(8,128)(2,1)S(1)} %collective-permute-done.16.refs_21_), channel_id=1, source_target_pairs={{0,32},{1,33},{2,34},{3,35},{4,36},{5,37},{6,38},{7,39},{8,40},{9,... | collective-permute-start | bytes 1572872 | tf_op jit(solution)/shard_map/ppermute | solution.py:135
  15.9 17.2 %collective-permute-start = (bf16[4,256,256]{2,1,0:T(8,128)(2,1)}, bf16[4,256,256]{2,1,0:T(8,128)(2,1)S(1)}, u32[]{:S(2)}, u32[]{:S(2)}) collective-permute-start(bf16[4,256,256]{2,1,0:T(8,128)(2,1)} %bitcast.6), channel_id=1, source_target_pairs={{0,4},{1,5},{2,6},{3,7},{4,8},{5,9},{6,10},{7,11},{8,12},{9,13},{1... | collective-permute-start | bytes 1572872 | tf_op jit(solution)/shard_map/ppermute | solution.py:135
  17.2 16.0 %collective-permute-start.1 = (bf16[4,256,256]{2,1,0:T(8,128)(2,1)}, bf16[4,256,256]{2,1,0:T(8,128)(2,1)S(1)}, u32[]{:S(2)}, u32[]{:S(2)}) collective-permute-start(bf16[4,256,256]{2,1,0:T(8,128)(2,1)} %bitcast.7), channel_id=1, source_target_pairs={{0,12},{1,13},{2,14},{3,15},{4,0},{5,1},{6,2},{7,3},{8,4},{9,5},{1... | collective-permute-start | bytes 1572872 | tf_op jit(solution)/shard_map/ppermute | solution.py:135
  22.0 11.6 %collective-permute-start.14 = (bf16[4,256,256]{2,1,0:T(8,128)(2,1)S(1)}, bf16[4,256,256]{2,1,0:T(8,128)(2,1)S(1)}, u32[]{:S(2)}, u32[]{:S(2)}) collective-permute-start(bf16[4,256,256]{2,1,0:T(8,128)(2,1)S(1)} %collective-permute-done.13.refs_18_), channel_id=1, source_target_pairs={{0,32},{1,33},{2,34},{3,35},{4,36},{5,37},{6,38},{7,39},{8,40},{9,... | collective-permute-start | bytes 1572872 | tf_op jit(solution)/shard_map/ppermute | solution.py:135
  27.6 11.2 %collective-permute-start.18 = (bf16[4,256,256]{2,1,0:T(8,128)(2,1)S(1)}, bf16[4,256,256]{2,1,0:T(8,128)(2,1)S(1)}, u32[]{:S(2)}, u32[]{:S(2)}) collective-permute-start(bf16[4,256,256]{2,1,0:T(8,128)(2,1)S(1)} %collective-permute-done.17.refs_22_), channel_id=1, source_target_pairs={{0,32},{1,33},{2,34},{3,35},{4,36},{5,37},{6,38},{7,39},{8,40},{9,... | collective-permute-start | bytes 1572872 | tf_op jit(solution)/shard_map/ppermute | solution.py:135
  30.7 13.1 %collective-permute-start.4 = (bf16[4,256,256]{2,1,0:T(8,128)(2,1)}, bf16[4,256,256]{2,1,0:T(8,128)(2,1)S(1)}, u32[]{:S(2)}, u32[]{:S(2)}) collective-permute-start(bf16[4,256,256]{2,1,0:T(8,128)(2,1)} %bitcast.8), channel_id=1, source_target_pairs={{0,3},{1,0},{2,1},{3,2},{4,7},{5,4},{6,5},{7,6},{8,11},{9,8},{10,9... | collective-permute-start | bytes 1572872 | tf_op jit(solution)/shard_map/ppermute | solution.py:135
  33.2 10.8 %collective-permute-start.3 = (bf16[4,256,256]{2,1,0:T(8,128)(2,1)}, bf16[4,256,256]{2,1,0:T(8,128)(2,1)S(1)}, u32[]{:S(2)}, u32[]{:S(2)}) collective-permute-start(bf16[4,256,256]{2,1,0:T(8,128)(2,1)} %bitcast.9), channel_id=1, source_target_pairs={{0,1},{1,2},{2,3},{3,0},{4,5},{5,6},{6,7},{7,4},{8,9},{9,10},{10,1... | collective-permute-start | bytes 1572872 | tf_op jit(solution)/shard_map/ppermute | solution.py:135
  33.3 40.3 %collective-permute-start.6 = (bf16[8,256,256]{2,1,0:T(8,128)(2,1)S(1)}, bf16[8,256,256]{2,1,0:T(8,128)(2,1)}, u32[]{:S(2)}, u32[]{:S(2)}) collective-permute-start(bf16[8,256,256]{2,1,0:T(8,128)(2,1)S(1)} %constant_dynamic-update-slice_fusion), channel_id=1, source_target_pairs={{0,1},{1,2},{2,3},{3,0},{4,5},{5,6},{6,7},{7,4},{8,9},{9,10},{10,1... | collective-permute-start | bytes 3145736 | tf_op jit(solution)/shard_map/ppermute | solution.py:135
  33.6 13.2 %collective-permute-start.15 = (bf16[4,256,256]{2,1,0:T(8,128)(2,1)S(1)}, bf16[4,256,256]{2,1,0:T(8,128)(2,1)S(1)}, u32[]{:S(2)}, u32[]{:S(2)}) collective-permute-start(bf16[4,256,256]{2,1,0:T(8,128)(2,1)S(1)} %collective-permute-done.14.refs_19_), channel_id=1, source_target_pairs={{0,32},{1,33},{2,34},{3,35},{4,36},{5,37},{6,38},{7,39},{8,40},{9,... | collective-permute-start | bytes 1572872 | tf_op jit(solution)/shard_map/ppermute | solution.py:135
  38.8 11.2 %collective-permute-start.19 = (bf16[4,256,256]{2,1,0:T(8,128)(2,1)S(1)}, bf16[4,256,256]{2,1,0:T(8,128)(2,1)S(1)}, u32[]{:S(2)}, u32[]{:S(2)}) collective-permute-start(bf16[4,256,256]{2,1,0:T(8,128)(2,1)S(1)} %collective-permute-done.18.refs_23_), channel_id=1, source_target_pairs={{0,32},{1,33},{2,34},{3,35},{4,36},{5,37},{6,38},{7,39},{8,40},{9,... | collective-permute-start | bytes 1572872 | tf_op jit(solution)/shard_map/ppermute | solution.py:135
  43.9 50.9 %collective-permute-start.20 = (bf16[16,256,256]{2,1,0:T(8,128)(2,1)}, bf16[16,256,256]{2,1,0:T(8,128)(2,1)S(1)}, u32[]{:S(2)}, u32[]{:S(2)}) collective-permute-start(bf16[16,256,256]{2,1,0:T(8,128)(2,1)} %pad_maximum_fusion), channel_id=1, source_target_pairs={{0,16},{1,17},{2,18},{3,19},{4,20},{5,21},{6,22},{7,23},{8,24},{9,... | collective-permute-start | bytes 6291464 | tf_op jit(solution)/shard_map/ppermute | solution.py:135
  46.8 26.9 %collective-permute-start.7 = (bf16[8,256,256]{2,1,0:T(8,128)(2,1)S(1)}, bf16[8,256,256]{2,1,0:T(8,128)(2,1)}, u32[]{:S(2)}, u32[]{:S(2)}) collective-permute-start(bf16[8,256,256]{2,1,0:T(8,128)(2,1)S(1)} %constant_dynamic-update-slice_fusion), channel_id=1, source_target_pairs={{0,3},{1,0},{2,1},{3,2},{4,7},{5,4},{6,5},{7,6},{8,11},{9,8},{10,9... | collective-permute-start | bytes 3145736 | tf_op jit(solution)/shard_map/ppermute | solution.py:135
  50.1 20.4 %collective-permute-start.5 = (bf16[4,256,256]{2,1,0:T(8,128)(2,1)S(1)}, bf16[4,256,256]{2,1,0:T(8,128)(2,1)S(1)}, u32[]{:S(2)}, u32[]{:S(2)}) collective-permute-start(bf16[4,256,256]{2,1,0:T(8,128)(2,1)S(1)} %collective-permute-done.4.refs_8_), channel_id=1, source_target_pairs={{0,3},{1,0},{2,1},{3,2},{4,7},{5,4},{6,5},{7,6},{8,11},{9,8},{10,9... | collective-permute-start | bytes 1572872 | tf_op jit(solution)/shard_map/ppermute | solution.py:135
  54.6 40.2 %collective-permute-start.21 = (bf16[12,256,256]{2,1,0:T(8,128)(2,1)}, bf16[12,256,256]{2,1,0:T(8,128)(2,1)}, u32[]{:S(2)}, u32[]{:S(2)}) collective-permute-start(bf16[12,256,256]{2,1,0:T(8,128)(2,1)} %pad_maximum_fusion.2), channel_id=1, source_target_pairs={{0,16},{1,17},{2,18},{3,19},{4,20},{5,21},{6,22},{7,23},{8,24},{9,... | collective-permute-start | bytes 4718600 | tf_op jit(solution)/shard_map/ppermute | solution.py:135
  73.6 21.2 %collective-permute-start.8 = (bf16[8,256,256]{2,1,0:T(8,128)(2,1)}, bf16[8,256,256]{2,1,0:T(8,128)(2,1)S(1)}, u32[]{:S(2)}, u32[]{:S(2)}) collective-permute-start(bf16[8,256,256]{2,1,0:T(8,128)(2,1)} %collective-permute-done.6.refs_10_), channel_id=1, source_target_pairs={{0,1},{1,2},{2,3},{3,0},{4,5},{5,6},{6,7},{7,4},{8,9},{9,10},{10,1... | collective-permute-start | bytes 3145736 | tf_op jit(solution)/shard_map/ppermute | solution.py:135
  73.7 21.1 %collective-permute-start.9 = (bf16[4,256,256]{2,1,0:T(8,128)(2,1)}, bf16[4,256,256]{2,1,0:T(8,128)(2,1)}, u32[]{:S(2)}, u32[]{:S(2)}) collective-permute-start(bf16[4,256,256]{2,1,0:T(8,128)(2,1)} %collective-permute-done.2.refs_6_), channel_id=1, source_target_pairs={{0,1},{1,2},{2,3},{3,0},{4,5},{5,6},{6,7},{7,4},{8,9},{9,10},{10,1... | collective-permute-start | bytes 1572872 | tf_op jit(solution)/shard_map/ppermute | solution.py:135
  80.0 14.7 %collective-permute-start.11 = (bf16[4,256,256]{2,1,0:T(8,128)(2,1)}, bf16[4,256,256]{2,1,0:T(8,128)(2,1)}, u32[]{:S(2)}, u32[]{:S(2)}) collective-permute-start(bf16[4,256,256]{2,1,0:T(8,128)(2,1)} %collective-permute-done.10.refs_14_), channel_id=1, source_target_pairs={{0,3},{1,0},{2,1},{3,2},{4,7},{5,4},{6,5},{7,6},{8,11},{9,8},{10,9... | collective-permute-start | bytes 1572872 | tf_op jit(solution)/shard_map/ppermute | solution.py:135
  117.8 11.7 %collective-permute-start.39 = (bf16[4,256,256]{2,1,0:T(8,128)(2,1)S(1)}, bf16[4,256,256]{2,1,0:T(8,128)(2,1)S(1)}, u32[]{:S(2)}, u32[]{:S(2)}) collective-permute-start(bf16[4,256,256]{2,1,0:T(8,128)(2,1)S(1)} %collective-permute-done.38.refs_21_), channel_id=1, source_target_pairs={{0,32},{1,33},{2,34},{3,35},{4,36},{5,37},{6,38},{7,39},{8,40},{9,... | collective-permute-start | bytes 1572872 | tf_op jit(solution)/shard_map/ppermute | solution.py:135
  117.9 15.1 %collective-permute-start.23 = (bf16[4,256,256]{2,1,0:T(8,128)(2,1)}, bf16[4,256,256]{2,1,0:T(8,128)(2,1)S(1)}, u32[]{:S(2)}, u32[]{:S(2)}) collective-permute-start(bf16[4,256,256]{2,1,0:T(8,128)(2,1)} %get-tuple-element.7.refs_3_), channel_id=1, source_target_pairs={{0,12},{1,13},{2,14},{3,15},{4,0},{5,1},{6,2},{7,3},{8,4},{9,5},{1... | collective-permute-start | bytes 1572872 | tf_op jit(solution)/shard_map/ppermute | solution.py:135
  119.7 15.1 %collective-permute-start.22 = (bf16[4,256,256]{2,1,0:T(8,128)(2,1)}, bf16[4,256,256]{2,1,0:T(8,128)(2,1)S(1)}, u32[]{:S(2)}, u32[]{:S(2)}) collective-permute-start(bf16[4,256,256]{2,1,0:T(8,128)(2,1)} %get-tuple-element.7.refs_3_), channel_id=1, source_target_pairs={{0,4},{1,5},{2,6},{3,7},{4,8},{5,9},{6,10},{7,11},{8,12},{9,13},{1... | collective-permute-start | bytes 1572872 | tf_op jit(solution)/shard_map/ppermute | solution.py:135
  123.9 12.3 %collective-permute-start.36 = (bf16[4,256,256]{2,1,0:T(8,128)(2,1)S(1)}, bf16[4,256,256]{2,1,0:T(8,128)(2,1)S(1)}, u32[]{:S(2)}, u32[]{:S(2)}) collective-permute-start(bf16[4,256,256]{2,1,0:T(8,128)(2,1)S(1)} %collective-permute-done.35.refs_18_), channel_id=1, source_target_pairs={{0,32},{1,33},{2,34},{3,35},{4,36},{5,37},{6,38},{7,39},{8,40},{9,... | collective-permute-start | bytes 1572872 | tf_op jit(solution)/shard_map/ppermute | solution.py:135
  129.5 11.2 %collective-permute-start.40 = (bf16[4,256,256]{2,1,0:T(8,128)(2,1)S(1)}, bf16[4,256,256]{2,1,0:T(8,128)(2,1)S(1)}, u32[]{:S(2)}, u32[]{:S(2)}) collective-permute-start(bf16[4,256,256]{2,1,0:T(8,128)(2,1)S(1)} %collective-permute-done.39.refs_22_), channel_id=1, source_target_pairs={{0,32},{1,33},{2,34},{3,35},{4,36},{5,37},{6,38},{7,39},{8,40},{9,... | collective-permute-start | bytes 1572872 | tf_op jit(solution)/shard_map/ppermute | solution.py:135
  132.9 13.2 %collective-permute-start.26 = (bf16[4,256,256]{2,1,0:T(8,128)(2,1)}, bf16[4,256,256]{2,1,0:T(8,128)(2,1)S(1)}, u32[]{:S(2)}, u32[]{:S(2)}) collective-permute-start(bf16[4,256,256]{2,1,0:T(8,128)(2,1)} %get-tuple-element.7.refs_3_), channel_id=1, source_target_pairs={{0,3},{1,0},{2,1},{3,2},{4,7},{5,4},{6,5},{7,6},{8,11},{9,8},{10,9... | collective-permute-start | bytes 1572872 | tf_op jit(solution)/shard_map/ppermute | solution.py:135
  132.9 13.5 %collective-permute-start.24 = (bf16[4,256,256]{2,1,0:T(8,128)(2,1)S(1)}, bf16[4,256,256]{2,1,0:T(8,128)(2,1)S(1)}, u32[]{:S(2)}, u32[]{:S(2)}) collective-permute-start(bf16[4,256,256]{2,1,0:T(8,128)(2,1)S(1)} %collective-permute-done.23.refs_5_), channel_id=1, source_target_pairs={{0,12},{1,13},{2,14},{3,15},{4,0},{5,1},{6,2},{7,3},{8,4},{9,5},{1... | collective-permute-start | bytes 1572872 | tf_op jit(solution)/shard_map/ppermute | solution.py:135
  134.9 27.9 %collective-permute-start.28 = (bf16[8,256,256]{2,1,0:T(8,128)(2,1)S(1)}, bf16[8,256,256]{2,1,0:T(8,128)(2,1)S(1)}, u32[]{:S(2)}, u32[]{:S(2)}) collective-permute-start(bf16[8,256,256]{2,1,0:T(8,128)(2,1)S(1)} %constant_dynamic-update-slice_fusion.2), channel_id=1, source_target_pairs={{0,1},{1,2},{2,3},{3,0},{4,5},{5,6},{6,7},{7,4},{8,9},{9,10},{10,1... | collective-permute-start | bytes 3145736 | tf_op jit(solution)/shard_map/ppermute | solution.py:135
  136.2 11.5 %collective-permute-start.37 = (bf16[4,256,256]{2,1,0:T(8,128)(2,1)S(1)}, bf16[4,256,256]{2,1,0:T(8,128)(2,1)S(1)}, u32[]{:S(2)}, u32[]{:S(2)}) collective-permute-start(bf16[4,256,256]{2,1,0:T(8,128)(2,1)S(1)} %collective-permute-done.36.refs_19_), channel_id=1, source_target_pairs={{0,32},{1,33},{2,34},{3,35},{4,36},{5,37},{6,38},{7,39},{8,40},{9,... | collective-permute-start | bytes 1572872 | tf_op jit(solution)/shard_map/ppermute | solution.py:135
  140.8 11.2 %collective-permute-start.41 = (bf16[4,256,256]{2,1,0:T(8,128)(2,1)S(1)}, bf16[4,256,256]{2,1,0:T(8,128)(2,1)S(1)}, u32[]{:S(2)}, u32[]{:S(2)}) collective-permute-start(bf16[4,256,256]{2,1,0:T(8,128)(2,1)S(1)} %collective-permute-done.40.refs_23_), channel_id=1, source_target_pairs={{0,32},{1,33},{2,34},{3,35},{4,36},{5,37},{6,38},{7,39},{8,40},{9,... | collective-permute-start | bytes 1572872 | tf_op jit(solution)/shard_map/ppermute | solution.py:135
  146.5 38.1 %collective-permute-start.42 = (bf16[16,256,256]{2,1,0:T(8,128)(2,1)S(1)}, bf16[16,256,256]{2,1,0:T(8,128)(2,1)S(1)}, u32[]{:S(2)}, u32[]{:S(2)}) collective-permute-start(bf16[16,256,256]{2,1,0:T(8,128)(2,1)S(1)} %pad_maximum_fusion.1), channel_id=1, source_target_pairs={{0,16},{1,17},{2,18},{3,19},{4,20},{5,21},{6,22},{7,23},{8,24},{9,... | collective-permute-start | bytes 6291464 | tf_op jit(solution)/shard_map/ppermute | solution.py:135
  155.8 26.7 %collective-permute-start.43 = (bf16[12,256,256]{2,1,0:T(8,128)(2,1)S(1)}, bf16[12,256,256]{2,1,0:T(8,128)(2,1)S(1)}, u32[]{:S(2)}, u32[]{:S(2)}) collective-permute-start(bf16[12,256,256]{2,1,0:T(8,128)(2,1)S(1)} %pad_maximum_fusion.3), channel_id=1, source_target_pairs={{0,16},{1,17},{2,18},{3,19},{4,20},{5,21},{6,22},{7,23},{8,24},{9,... | collective-permute-start | bytes 4718600 | tf_op jit(solution)/shard_map/ppermute | solution.py:135
  158.2 14.7 %collective-permute-start.29 = (bf16[8,256,256]{2,1,0:T(8,128)(2,1)S(1)}, bf16[8,256,256]{2,1,0:T(8,128)(2,1)S(1)}, u32[]{:S(2)}, u32[]{:S(2)}) collective-permute-start(bf16[8,256,256]{2,1,0:T(8,128)(2,1)S(1)} %constant_dynamic-update-slice_fusion.2), channel_id=1, source_target_pairs={{0,3},{1,0},{2,1},{3,2},{4,7},{5,4},{6,5},{7,6},{8,11},{9,8},{10,9... | collective-permute-start | bytes 3145736 | tf_op jit(solution)/shard_map/ppermute | solution.py:135
  162.8 19.6 %collective-permute-start.30 = (bf16[8,256,256]{2,1,0:T(8,128)(2,1)S(1)}, bf16[8,256,256]{2,1,0:T(8,128)(2,1)S(1)}, u32[]{:S(2)}, u32[]{:S(2)}) collective-permute-start(bf16[8,256,256]{2,1,0:T(8,128)(2,1)S(1)} %collective-permute-done.28.refs_10_), channel_id=1, source_target_pairs={{0,1},{1,2},{2,3},{3,0},{4,5},{5,6},{6,7},{7,4},{8,9},{9,10},{10,1... | collective-permute-start | bytes 3145736 | tf_op jit(solution)/shard_map/ppermute | solution.py:135
  (51 other events, 743.2 us)
